TPU v7x, 512 devices: a whole 4x4x16 slice. The times are simulated.
512 devices in a mesh: sub: 32 (over z, core), mem: 16 (over x, y).
Axes of the slice: x: 4, y: 4, z: 16, core: 2. Of those that a mesh axis runs over, the one named last changes fastest.
Arguments:
- dechirped_echo_matrix: bfloat16 [32, 2, 256, 8192], P('sub', None, 'mem'), may hold values from -6 to 6
- bearing_rotation_table: float32 [32, 16, 512, 256], P('sub', 'mem'), may hold values from -3.140625 to 3.140625
- patch_subset_holder: int32 [32, 16, 16], P('sub', 'mem'), may hold values from 0 to 31, as said below
- modulation_slope: float32 [32, 16, 2, 16], P('sub', 'mem'), may hold values from -0.5 to 0.5
- regrid_lead_cell: int32 [32, 16, 2, 128], P('sub', 'mem'), may hold values from 0 to 124
- regrid_weight: float32 [32, 16, 2, 128], P('sub', 'mem'), may hold values from 0 to 1
Outputs:
- ground_image: bfloat16 [512, 2, 128, 128], P(('sub', 'mem'))
Inputs may be any that keep to these rules, and one draw needn't show every extreme that they name: `patch_subset_holder`: each group and sector sends at most 2 of its 16 blocks to any one tile; in every sector some tile receives exactly 2 blocks from every group.
All inputs are finite; a program needn't handle non-finite values.
Results may differ from a plain program's by a relative error of at most 0.014.
Values may be sent and summed in bfloat16 or wider, within the bound.
No kernel may reach another device: no remote copies, remote signals or barrier semaphores. Data moves between devices by JAX's collectives and lax.ppermute only.
A program may use at most 64 MiB of HBM per device.

v0:
```python
import math
import jax
import jax.numpy as jnp
from jax import lax
from jax.sharding import PartitionSpec as P

FREQUENCIES = 8192
FIRST_RADIX = 64
SECOND_RADIX = 128
SWEEPS = 256
ANGLES = 512
BLOCK_SIDE = 128


def dft_tables(length):
    positions = jnp.arange(length, dtype=jnp.int32)
    turns = positions[:, None] * positions[None, :] % length
    phase_angle = turns.astype(jnp.float32) * (2.0 * math.pi / length)
    return jnp.stack([jnp.cos(phase_angle), jnp.sin(phase_angle)]).astype(jnp.bfloat16)


def twiddle(row_count, column_count, length):
    row_index = jnp.arange(row_count, dtype=jnp.int32)
    column_index = jnp.arange(column_count, dtype=jnp.int32)
    turns = row_index[:, None] * column_index[None, :] % length
    phase_angle = turns.astype(jnp.float32) * (2.0 * math.pi / length)
    return (jnp.cos(phase_angle), jnp.sin(phase_angle))


def combine(product):
    return (product[0, 0] - product[1, 1], product[0, 1] + product[1, 0])


def range_transform(sweeps):
    sweep_count = sweeps.shape[1]
    reshaped = sweeps.reshape(2, sweep_count, FIRST_RADIX, SECOND_RADIX)
    product = jnp.einsum(
        "qrk,pskj->qpsrj", dft_tables(FIRST_RADIX), reshaped, preferred_element_type=jnp.float32
    )
    inphase_part, quadrature_part = combine(product)
    cosine, sine_part = twiddle(FIRST_RADIX, SECOND_RADIX, FREQUENCIES)
    turned = jnp.stack(
        [
            inphase_part * cosine - quadrature_part * sine_part,
            inphase_part * sine_part + quadrature_part * cosine,
        ]
    ).astype(jnp.bfloat16)
    product = jnp.einsum(
        "quj,psrj->qpsur", dft_tables(SECOND_RADIX), turned, preferred_element_type=jnp.float32
    )
    inphase_part, quadrature_part = combine(product)
    factor = 1.0 / math.sqrt(FREQUENCIES)
    return (
        (jnp.stack([inphase_part, quadrature_part]) * factor)
        .astype(jnp.bfloat16)
        .reshape(2, sweep_count, FREQUENCIES)
    )


def phase_tables(angles):
    factor = 1.0 / math.sqrt(SWEEPS)
    return jnp.stack([jnp.cos(angles) * factor, jnp.sin(angles) * factor]).astype(jnp.bfloat16)


def strip_modulation(
    inphase_part, quadrature_part, modulation_line_entries, tilt_patches, slant_patches
):
    tilt_linear_slope = modulation_line_entries[0].reshape(tilt_patches, slant_patches)
    slant_linear_slope = modulation_line_entries[1].reshape(tilt_patches, slant_patches)
    positions = jnp.arange(BLOCK_SIDE, dtype=jnp.float32)
    phase_angle = (
        tilt_linear_slope[:, None, :, None] * positions[None, :, None, None]
        + slant_linear_slope[:, None, :, None] * positions[None, None, None, :]
    )
    cosine = jnp.cos(phase_angle)
    sine_part = jnp.sin(phase_angle)
    inphase_part = inphase_part.reshape(tilt_patches, BLOCK_SIDE, slant_patches, BLOCK_SIDE)
    quadrature_part = quadrature_part.reshape(tilt_patches, BLOCK_SIDE, slant_patches, BLOCK_SIDE)
    return jnp.stack(
        [
            inphase_part * cosine - quadrature_part * sine_part,
            inphase_part * sine_part + quadrature_part * cosine,
        ]
    ).astype(jnp.bfloat16)


def stencil(offsets, fractions):
    weights = [
        -fractions * (fractions - 1.0) * (fractions - 2.0) / 6.0,
        (fractions + 1.0) * (fractions - 1.0) * (fractions - 2.0) / 2.0,
        -(fractions + 1.0) * fractions * (fractions - 2.0) / 2.0,
        (fractions + 1.0) * fractions * (fractions - 1.0) / 6.0,
    ]
    sources = jnp.arange(fractions.shape[-1], dtype=jnp.int32)
    distance = sources - offsets[..., None]
    weights_sum = jnp.zeros(distance.shape, jnp.float32)
    for stencil_tap in range(4):
        weights_sum = weights_sum + jnp.where(
            distance == stencil_tap, weights[stencil_tap][..., None], jnp.float32(0.0)
        )
    return weights_sum.astype(jnp.bfloat16)


def on_device(
    dechirped_echo_matrix,
    bearing_rotation_table,
    patch_subset_holder,
    modulation_slope,
    regrid_lead_cell,
    regrid_weight,
):
    groups = lax.axis_size("sub")
    members = lax.axis_size("mem")
    sector = FREQUENCIES // members
    tilt_patches = ANGLES // BLOCK_SIDE
    slant_patches = sector // BLOCK_SIDE
    block_count = tilt_patches * slant_patches
    capacity = max(2, 2 * block_count // groups)
    spectrum = range_transform(dechirped_echo_matrix[0])
    sweep_count = spectrum.shape[1]
    by_sector = spectrum.reshape(2, sweep_count, members, sector)
    tables = phase_tables(bearing_rotation_table[0, 0])
    product = jnp.einsum(
        "qas,psc->qpac",
        tables,
        lax.all_to_all(by_sector, "mem", split_axis=2, concat_axis=1, tiled=True)[:, :, 0, :],
        preferred_element_type=jnp.float32,
    )
    inphase_part, quadrature_part = combine(product)
    focused_image = jnp.stack([inphase_part, quadrature_part])[:, :, None, :]
    patch_list = strip_modulation(
        focused_image[0, :, 0, :],
        focused_image[1, :, 0, :],
        modulation_slope[0, 0],
        tilt_patches,
        slant_patches,
    )
    own_tables = stencil(regrid_lead_cell[0, 0], regrid_weight[0, 0])
    owners = patch_subset_holder[0, 0]
    onehot = owners[:, None] == jnp.arange(groups, dtype=jnp.int32)[None, :]
    counts = onehot.astype(jnp.int32)
    before = jnp.cumsum(counts, axis=0) - counts
    rank_within = jnp.sum(before * counts, axis=1)
    slot_index = owners * capacity + rank_within
    selector = (
        slot_index[None, :] == jnp.arange(groups * capacity, dtype=jnp.int32)[:, None]
    ).astype(jnp.bfloat16)
    selector = selector.reshape(groups * capacity, tilt_patches, slant_patches)
    packed = jnp.einsum(
        "kAC,pAaCc->kpac", selector, patch_list, preferred_element_type=jnp.float32
    ).astype(jnp.bfloat16)
    packed = packed.reshape(groups, capacity, 2, BLOCK_SIDE, BLOCK_SIDE)
    rows_done = jnp.einsum(
        "ya,skpac->skpyc",
        own_tables[0],
        lax.all_to_all(packed, "sub", split_axis=0, concat_axis=0, tiled=True),
        preferred_element_type=jnp.float32,
    ).astype(jnp.bfloat16)
    interpolated = jnp.einsum(
        "skpyc,xc->skpyx", rows_done, own_tables[1], preferred_element_type=jnp.float32
    )
    per_source = lax.optimization_barrier(jnp.sum(interpolated, axis=1).astype(jnp.bfloat16))
    ground = jnp.sum(per_source.astype(jnp.float32), axis=0)
    return (0.25 * ground).astype(jnp.bfloat16)[None]


def solution(mesh):
    return jax.shard_map(
        on_device,
        mesh=mesh,
        in_specs=(
            P("sub", None, "mem", None),
            P("sub", "mem", None, None),
            P("sub", "mem", None),
            P("sub", "mem", None, None),
            P("sub", "mem", None, None),
            P("sub", "mem", None, None),
        ),
        out_specs=P(("sub", "mem"), None, None, None),
        check_vma=False,
    )
```

profile of v0, /device:TPU:32, one launch (start us, length us, event | category | flops | bytes accessed | tf_op | source)
XLA Modules:
  0.0 251.5 jit_solution(1296951972144069994)
XLA Ops:
  0.0 0.2 sine_convert_fusion.1
  0.2 0.1 fusion.59
  0.3 0.3 sine_convert_fusion
  0.6 1.2 copy.78
  1.8 0.4 convolution_bitcast_fusion.2
  2.2 0.2 subtract_convert_fusion
  2.4 0.4 convolution_bitcast_fusion.1
  2.8 0.2 slice_subtract_fusion.1
  3.0 0.3 copy.53
  3.4 0.0 copy-start.4
  3.4 0.0 copy-start.1
  3.4 0.0 copy-start
  3.4 0.3 add.211
  3.7 0.3 copy.52
  4.0 0.3 sub.102
  4.3 0.1 fusion.22
  4.4 1.1 copy.54
  5.5 7.0 %all-to-all-start = ((bf16[2,16,16,512]{3,1,0,2:T(8,128)(2,1)}), bf16[2,16,16,512]{3,1,0,2:T(8,128)(2,1)S(1)}, u32[]{:S(2)}, u32[]{:S(2)}) async-start(bf16[2,16,16,512]{3,1,0,2:T(8,128)(2,1)} %copy.54), calls=%async_computation | async-start | bytes 1048576 | tf_op jit(solution)/shard_map/all_to_all | solution.py:126
  12.6 0.0 copy-done.4
  12.6 0.1 mul.445
  12.7 0.1 iota_multiply_fusion
  12.8 0.0 copy-done.1
  12.8 0.1 fusion.61
  12.9 0.2 select_reduce_fusion
  13.1 0.1 mul.441
  13.2 0.1 reduce_sum.30
  13.2 0.1 mul.412
  13.3 0.1 iota_multiply_fusion.1
  13.4 0.0 copy-done
  13.4 1.9 fusion.30
  15.3 8.7 %all-to-all-done = bf16[2,16,16,512]{3,1,0,2:T(8,128)(2,1)S(1)} async-done(((bf16[2,16,16,512]{3,1,0,2:T(8,128)(2,1)}), bf16[2,16,16,512]{3,1,0,2:T(8,128)(2,1)S(1)}, u32[]{:S(2)}, u32[]{:S(2)}) %all-to-all-start) | async-done | bytes 524320 | tf_op jit(solution)/shard_map/all_to_all | solution.py:126
  24.1 0.8 convolution_bitcast_fusion
  24.9 0.5 slice_subtract_fusion
  25.3 0.8 copy.57
  26.1 0.8 copy.59
  26.9 4.6 %fusion.19 = (bf16[1,4,128,4,128]{4,2,3,1,0:T(8,128)(2,1)S(1)}, bf16[1,4,128,4,128]{4,2,3,1,0:T(8,128)(2,1)S(1)}) fusion(f32[1,4,128,4,128]{4,3,0,2,1:T(4,128)S(1)} %bitcast.122, f32[1,4,128,4,128]{4,3,0,2,1:T(4,128)S(1)} %bitcast.121, f32[4,4,128]{2,1,0:T(4,128)S(1)} %iota_multiply_fusion, f32[4,128,4]{1,2,0:T(4,128)S(1)} %iota_multiply_fusion.1), kind=kLoop, calls=%fused_computation.18 | loop fusion | flops 2359296 | bytes 3162112 | tf_op jit(solution)/shard_map/convert
  31.6 0.1 pad_maximum_fusion
  31.7 1.9 bitcast_convert_fusion
  33.6 6.6 %copy.64 = bf16[32,2,2,128,128]{4,1,3,2,0:T(2,128)(2,1)} copy(bf16[32,2,2,128,128]{4,1,0,3,2:T(2,128)(2,1)S(1)} %bitcast.123) | data formatting | bytes 8388608 | tf_op jit(solution)/shard_map/reshape | solution.py:152
  40.2 0.0 copy-start.3
  40.2 15.5 %all-to-all-start.1 = ((bf16[32,2,2,128,128]{4,1,3,2,0:T(2,128)(2,1)}), bf16[32,2,2,128,128]{4,1,3,2,0:T(2,128)(2,1)}, u32[]{:S(2)}, u32[]{:S(2)}) async-start(bf16[32,2,2,128,128]{4,1,3,2,0:T(2,128)(2,1)} %copy.64), calls=%async_computation.1 | async-start | bytes 8388608 | tf_op jit(solution)/shard_map/all_to_all | solution.py:156
  55.8 0.0 copy-done.3
  55.8 0.0 copy-done.2
  55.8 0.2 add_convert_fusion.1
  56.0 189.5 %all-to-all-done.1 = bf16[32,2,2,128,128]{4,1,3,2,0:T(2,128)(2,1)} async-done(((bf16[32,2,2,128,128]{4,1,3,2,0:T(2,128)(2,1)}), bf16[32,2,2,128,128]{4,1,3,2,0:T(2,128)(2,1)}, u32[]{:S(2)}, u32[]{:S(2)}) %all-to-all-start.1) | async-done | bytes 4194336 | tf_op jit(solution)/shard_map/all_to_all | solution.py:156
  245.5 5.0 %fusion.9 = bf16[32,2,128,128]{3,2,1,0:T(8,128)(2,1)S(1)} fusion(bf16[32,2,2,128,128]{4,1,3,2,0:T(2,128)(2,1)} %all-to-all-done.1, bf16[2,128,128]{2,1,0:T(8,128)(2,1)S(1)} %add_convert_fusion.1), kind=kOutput, calls=%fused_computation.7 | convolution fusion | flops 1076887552 | bytes 6356992 | tf_op jit(solution)/shard_map/skpyc,xc->skpyx/dot_general | solution.py:159
  250.5 0.3 convert_reduce_fusion
  250.8 0.6 fusion.39
  (7 shorter events, 0.1 us)
Async XLA Ops:
  3.4 9.2 %copy-start.4 = (f32[1,1,2,16]{3,2,1,0:T(2,128)S(1)}, f32[1,1,2,16]{3,2,1,0:T(2,128)}, u32[]{:S(2)}) copy-start(f32[1,1,2,16]{3,2,1,0:T(2,128)} %param.9) | copy-start | bytes 388
  3.4 9.4 %copy-start.1 = (s32[1,1,16]{2,1,0:T(1,128)S(1)}, s32[1,1,16]{2,1,0:T(1,128)}, u32[]{:S(2)}) copy-start(s32[1,1,16]{2,1,0:T(1,128)} %param.8) | copy-start | bytes 196
  3.4 10.0 %copy-start = (f32[1,1,512,256]{3,2,1,0:T(8,128)S(1)}, f32[1,1,512,256]{3,2,1,0:T(8,128)}, u32[]{:S(2)}) copy-start(f32[1,1,512,256]{3,2,1,0:T(8,128)} %param.7) | copy-start | bytes 1572868
  5.5 18.5 %all-to-all-start = ((bf16[2,16,16,512]{3,1,0,2:T(8,128)(2,1)}), bf16[2,16,16,512]{3,1,0,2:T(8,128)(2,1)S(1)}, u32[]{:S(2)}, u32[]{:S(2)}) async-start(bf16[2,16,16,512]{3,1,0,2:T(8,128)(2,1)} %copy.54), calls=%async_computation | async-start | bytes 1048576 | tf_op jit(solution)/shard_map/all_to_all | solution.py:126
  40.2 15.6 %copy-start.3 = (f32[1,1,2,128]{3,2,1,0:T(2,128)S(1)}, f32[1,1,2,128]{3,2,1,0:T(2,128)}, u32[]{:S(2)}) copy-start(f32[1,1,2,128]{3,2,1,0:T(2,128)} %param.11) | copy-start | bytes 3076
  40.2 15.6 %copy-start.2 = (s32[1,1,2,128]{3,2,1,0:T(2,128)S(1)}, s32[1,1,2,128]{3,2,1,0:T(2,128)}, u32[]{:S(2)}) copy-start(s32[1,1,2,128]{3,2,1,0:T(2,128)} %param.10) | copy-start | bytes 3076
  40.2 205.3 %all-to-all-start.1 = ((bf16[32,2,2,128,128]{4,1,3,2,0:T(2,128)(2,1)}), bf16[32,2,2,128,128]{4,1,3,2,0:T(2,128)(2,1)}, u32[]{:S(2)}, u32[]{:S(2)}) async-start(bf16[32,2,2,128,128]{4,1,3,2,0:T(2,128)(2,1)} %copy.64), calls=%async_computation.1 | async-start | bytes 8388608 | tf_op jit(solution)/shard_map/all_to_all | solution.py:156
where the time goes:
time: 252 us; the launch traced here: 251 us
  waiting for transfers between devices  198 us (79%)
  starting transfers between devices  22.6 us (9%)
  local copies, waits for them, and re-layouts  12.1 us (5%)
  other arithmetic  9.92 us (4%)
  matrix products  8.43 us (3%)
    all_to_all x1, waiting for transfers between devices, on_device(): lax.all_to_all(packed, 'sub', split_axis=0, concat_axis=0, tiled=True)  189 us
    all_to_all x1, starting transfers between devices, on_device(): lax.all_to_all(packed, 'sub', split_axis=0, concat_axis=0, tiled=True)  15.5 us
    all_to_all x1, waiting for transfers between devices, on_device(): lax.all_to_all(by_sector, 'mem', split_axis=2, concat_axis=1, tiled=True)  8.73 us
    all_to_all x1, starting transfers between devices, on_device(): lax.all_to_all(by_sector, 'mem', split_axis=2, concat_axis=1, tiled=True)  7.04 us
    reshape x1, local copies, waits for them, and re-layouts, on_device(): packed = packed.reshape(groups, capacity, 2, BLOCK_SIDE, BLOCK_SIDE)  6.62 us
    another operation x4, other arithmetic  5.31 us
  transfers between devices with their start and end apart: 2, of which 2 were waited for; matrix products, arithmetic and copies ran while one was open for 1% of the time, Pallas kernels for 0%

commit v1 on v0

--- a/solution.py
+++ b/solution.py
@@ -123,7 +123,12 @@
     product = jnp.einsum(
         "qas,psc->qpac",
         tables,
-        lax.all_to_all(by_sector, "mem", split_axis=2, concat_axis=1, tiled=True)[:, :, 0, :],
+        jnp.concatenate(
+            lax.all_to_all(
+                jnp.stack(jnp.split(by_sector, lax.axis_size("mem"), axis=2)), "mem", 0, 0
+            ),
+            axis=1,
+        )[:, :, 0, :],
         preferred_element_type=jnp.float32,
     )
     inphase_part, quadrature_part = combine(product)

time: 252 us -> 268 us (1.063)
  local copies, waits for them, and re-layouts: 12.1 us -> 26.6 us
    unnamed x11 -> x26, local copies, waits for them, and re-layouts: 1.18 us -> 10.3 us
    reshape x1, local copies, waits for them, and re-layouts: 6.62 us -> 11.4 us  [on_device(): packed = packed.reshape(groups, capacity, 2, BLOCK_SIDE, BLOCK_SIDE)]
where the time goes in v1:
time: 268 us
  waiting for transfers between devices  198 us (74%)
  local copies, waits for them, and re-layouts  26.6 us (10%)
  starting transfers between devices  22.6 us (8%)
  matrix products  10.3 us (4%)
  other arithmetic  9.92 us (4%)
    all_to_all x1, waiting for transfers between devices, on_device(): lax.all_to_all(packed, 'sub', split_axis=0, concat_axis=0, tiled=True)  189 us
    all_to_all x1, starting transfers between devices, on_device(): lax.all_to_all(packed, 'sub', split_axis=0, concat_axis=0, tiled=True)  15.5 us
    reshape x1, local copies, waits for them, and re-layouts, on_device(): packed = packed.reshape(groups, capacity, 2, BLOCK_SIDE, BLOCK_SIDE)  11.4 us
    unnamed x26, local copies, waits for them, and re-layouts  10.3 us
    all_to_all x1, waiting for transfers between devices, on_device(): lax.all_to_all(jnp.stack(jnp.split(by_sector, lax.axis_size('mem'), axis=...  8.74 us
    all_to_all x1, starting transfers between devices, on_device(): lax.all_to_all(jnp.stack(jnp.split(by_sector, lax.axis_size('mem'), axis=...  7.04 us
  transfers between devices with their start and end apart: 2, of which 2 were waited for; matrix products, arithmetic and copies ran while one was open for 1% of the time, Pallas kernels for 0%

profile of v1, /device:TPU:32, one launch (start us, length us, event | category | flops | bytes accessed | tf_op | source)
XLA Modules:
  0.0 267.9 jit_solution(12341329965060275157)
XLA Ops:
  0.0 0.2 sine_convert_fusion.1
  0.2 0.1 fusion.53
  0.3 0.3 sine_convert_fusion
  0.6 1.2 copy.346
  1.8 0.4 convolution_bitcast_fusion.2
  2.2 0.2 subtract_convert_fusion
  2.4 0.4 convolution_bitcast_fusion.1
  2.8 0.2 slice_subtract_fusion.1
  3.0 0.3 copy.307
  3.4 0.3 add.211
  3.6 0.3 copy.306
  4.0 0.3 sub.102
  4.3 0.1 fusion.16
  4.4 1.1 fusion.72
  5.6 0.6 constant_dynamic-update-slice_fusion.15
  6.2 0.6 constant_dynamic-update-slice_fusion.14
  6.8 0.6 constant_dynamic-update-slice_fusion.13
  7.4 0.6 constant_dynamic-update-slice_fusion.12
  8.0 0.6 constant_dynamic-update-slice_fusion.11
  8.6 0.6 constant_dynamic-update-slice_fusion.10
  9.2 0.6 constant_dynamic-update-slice_fusion.9
  9.8 0.6 constant_dynamic-update-slice_fusion.8
  10.5 0.6 constant_dynamic-update-slice_fusion.7
  11.1 0.6 constant_dynamic-update-slice_fusion.6
  11.7 0.6 constant_dynamic-update-slice_fusion.5
  12.3 0.6 constant_dynamic-update-slice_fusion.4
  12.9 0.6 constant_dynamic-update-slice_fusion.3
  13.5 0.6 constant_dynamic-update-slice_fusion.2
  14.1 0.6 constant_dynamic-update-slice_fusion.1
  14.7 0.6 constant_dynamic-update-slice_fusion
  15.3 7.0 %all-to-all-start = ((bf16[16,2,16,1,512]{4,2,1,3,0:T(8,128)(2,1)}), bf16[16,2,16,1,512]{4,2,1,3,0:T(8,128)(2,1)S(1)}, u32[]{:S(2)}, u32[]{:S(2)}) async-start(bf16[16,2,16,1,512]{4,2,1,3,0:T(8,128)(2,1)} %constant_dynamic-update-slice_fusion), calls=%async_computation | async-start | bytes 1048576 | tf_op jit(solution)/shard_map/all_to_all | solution.py:127
  22.7 0.2 select_reduce_fusion
  23.2 1.9 fusion.24
  25.1 8.7 %all-to-all-done = bf16[16,2,16,1,512]{4,2,1,3,0:T(8,128)(2,1)S(1)} async-done(((bf16[16,2,16,1,512]{4,2,1,3,0:T(8,128)(2,1)}), bf16[16,2,16,1,512]{4,2,1,3,0:T(8,128)(2,1)S(1)}, u32[]{:S(2)}, u32[]{:S(2)}) %all-to-all-start) | async-done | bytes 524320 | tf_op jit(solution)/shard_map/all_to_all | solution.py:127
  33.9 0.8 convolution_bitcast_fusion
  34.7 0.5 slice_subtract_fusion
  35.2 0.8 copy.310
  36.0 0.8 copy.312
  36.8 4.6 %fusion.13 = (bf16[1,4,128,4,128]{4,2,3,1,0:T(8,128)(2,1)S(1)}, bf16[1,4,128,4,128]{4,2,3,1,0:T(8,128)(2,1)S(1)}) fusion(f32[1,4,128,4,128]{4,3,0,2,1:T(4,128)S(1)} %bitcast.152, f32[1,4,128,4,128]{4,3,0,2,1:T(4,128)S(1)} %bitcast.151, f32[4,4,128]{2,1,0:T(4,128)S(1)} %iota_multiply_fusion, f32[4,128,4]{1,2,0:T(4,128)S(1)} %iota_multiply_fusion.1), kind=kLoop, calls=%fused_computation.17 | loop fusion | flops 2359296 | bytes 3162112 | tf_op jit(solution)/shard_map/convert
  41.4 0.1 pad_maximum_fusion
  41.5 3.8 %bitcast_convert_fusion = bf16[64,2,128,128]{3,0,2,1:T(8,128)(2,1)} fusion(bf16[2,4,128,4,128]{4,2,3,1,0:T(8,128)(2,1)S(1)} %pad_maximum_fusion, s32[4,4]{1,0:T(4,128)S(1)} %add.203), kind=kOutput, calls=%fused_computation | convolution fusion | flops 69207040 | bytes 5242944 | tf_op jit(solution)/shard_map/kAC,pAaCc->kpac/dot_general | solution.py:154
  45.4 11.4 %copy.317 = bf16[32,2,2,128,128]{3,4,2,1,0:T(8,128)(2,1)} copy(bf16[32,2,2,128,128]{4,1,0,3,2:T(2,128)(2,1)} %bitcast.153) | data formatting | bytes 8388608 | tf_op jit(solution)/shard_map/reshape | solution.py:157
  56.7 15.5 %all-to-all-start.1 = ((bf16[32,2,2,128,128]{3,4,2,1,0:T(8,128)(2,1)}), bf16[32,2,2,128,128]{3,4,2,1,0:T(8,128)(2,1)}, u32[]{:S(2)}, u32[]{:S(2)}) async-start(bf16[32,2,2,128,128]{3,4,2,1,0:T(8,128)(2,1)} %copy.317), calls=%async_computation.1 | async-start | bytes 8388608 | tf_op jit(solution)/shard_map/all_to_all | solution.py:161
  72.3 0.2 add_convert_fusion.1
  72.5 189.5 %all-to-all-done.1 = bf16[32,2,2,128,128]{3,4,2,1,0:T(8,128)(2,1)} async-done(((bf16[32,2,2,128,128]{3,4,2,1,0:T(8,128)(2,1)}), bf16[32,2,2,128,128]{3,4,2,1,0:T(8,128)(2,1)}, u32[]{:S(2)}, u32[]{:S(2)}) %all-to-all-start.1) | async-done | bytes 4194336 | tf_op jit(solution)/shard_map/all_to_all | solution.py:161
  262.0 4.9 %fusion.5 = bf16[32,2,128,128]{3,2,1,0:T(8,128)(2,1)S(1)} fusion(bf16[32,2,2,128,128]{3,4,2,1,0:T(8,128)(2,1)} %all-to-all-done.1, bf16[2,128,128]{2,1,0:T(8,128)(2,1)S(1)} %add_convert_fusion.1), kind=kOutput, calls=%fused_computation.6 | convolution fusion | flops 1076887552 | bytes 6356992 | tf_op jit(solution)/shard_map/skpyc,xc->skpyx/dot_general | solution.py:164
  266.9 0.3 convert_reduce_fusion
  267.3 0.6 fusion.33
  (23 shorter events, 0.7 us)
Async XLA Ops:
  4.0 18.4 %copy-start.4 = (f32[1,1,2,16]{3,2,1,0:T(2,128)S(1)}, f32[1,1,2,16]{3,2,1,0:T(2,128)}, u32[]{:S(2)}) copy-start(f32[1,1,2,16]{3,2,1,0:T(2,128)} %param.9) | copy-start | bytes 388
  4.0 18.6 %copy-start.1 = (s32[1,1,16]{2,1,0:T(1,128)S(1)}, s32[1,1,16]{2,1,0:T(1,128)}, u32[]{:S(2)}) copy-start(s32[1,1,16]{2,1,0:T(1,128)} %param.8) | copy-start | bytes 196
  4.0 19.2 %copy-start = (f32[1,1,512,256]{3,2,1,0:T(8,128)S(1)}, f32[1,1,512,256]{3,2,1,0:T(8,128)}, u32[]{:S(2)}) copy-start(f32[1,1,512,256]{3,2,1,0:T(8,128)} %param.7) | copy-start | bytes 1572868
  15.3 18.5 %all-to-all-start = ((bf16[16,2,16,1,512]{4,2,1,3,0:T(8,128)(2,1)}), bf16[16,2,16,1,512]{4,2,1,3,0:T(8,128)(2,1)S(1)}, u32[]{:S(2)}, u32[]{:S(2)}) async-start(bf16[16,2,16,1,512]{4,2,1,3,0:T(8,128)(2,1)} %constant_dynamic-update-slice_fusion), calls=%async_computation | async-start | bytes 1048576 | tf_op jit(solution)/shard_map/all_to_all | solution.py:127
  56.7 15.5 %copy-start.3 = (f32[1,1,2,128]{3,2,1,0:T(2,128)S(1)}, f32[1,1,2,128]{3,2,1,0:T(2,128)}, u32[]{:S(2)}) copy-start(f32[1,1,2,128]{3,2,1,0:T(2,128)} %param.11) | copy-start | bytes 3076
  56.7 15.6 %copy-start.2 = (s32[1,1,2,128]{3,2,1,0:T(2,128)S(1)}, s32[1,1,2,128]{3,2,1,0:T(2,128)}, u32[]{:S(2)}) copy-start(s32[1,1,2,128]{3,2,1,0:T(2,128)} %param.10) | copy-start | bytes 3076
  56.7 205.3 %all-to-all-start.1 = ((bf16[32,2,2,128,128]{3,4,2,1,0:T(8,128)(2,1)}), bf16[32,2,2,128,128]{3,4,2,1,0:T(8,128)(2,1)}, u32[]{:S(2)}, u32[]{:S(2)}) async-start(bf16[32,2,2,128,128]{3,4,2,1,0:T(8,128)(2,1)} %copy.317), calls=%async_computation.1 | async-start | bytes 8388608 | tf_op jit(solution)/shard_map/all_to_all | solution.py:161
